TPU v7x, 128 devices: a whole 4x4x4 slice. The times are simulated.
128 devices in a mesh: seq: 32 (over x, z, core), head: 4 (over y).
Axes of the slice: x: 4, y: 4, z: 4, core: 2. Of those that a mesh axis runs over, the one named last changes fastest.
Arguments:
- tokens: bfloat16 [16384, 1024], P('seq'), may hold values from -6 to 6
- segment_ids: int32 [16384], replicated, may hold values from 0 to 4, as said below
- mix_gain: float32 [1024], replicated, may hold values from 0.1 to 1.9
- in_weight: bfloat16 [1024, 3, 1024], P(None, None, 'head'), may hold values from -0.1875 to 0.1875
- conv_weight: bfloat16 [3, 1024], P(None, 'head'), may hold values from -3 to 3
- out_weight: bfloat16 [1024, 1024], P(None, 'head'), may hold values from -0.1875 to 0.1875
- ffn_gain: float32 [1024], replicated, may hold values from 0.1 to 1.9
- gate_weight: bfloat16 [1024, 4608], P(None, 'head'), may hold values from -0.1875 to 0.1875
- up_weight: bfloat16 [1024, 4608], P(None, 'head'), may hold values from -0.1875 to 0.1875
- down_weight: bfloat16 [1024, 4608], P(None, 'head'), may hold values from -0.125 to 0.125
- cotangent: bfloat16 [16384, 1024], P('seq'), may hold values from -6 to 6
Outputs:
- result: bfloat16 [16384, 1024], P('seq')
- grad_tokens: float32 [16384, 1024], P('seq')
- grad_mix_gain: float32 [1024], replicated
- grad_in_weight: float32 [1024, 3, 1024], P('seq', None, 'head')
- grad_conv_weight: float32 [3, 1024], P(None, 'head')
- grad_out_weight: float32 [1024, 1024], P('seq', 'head')
- grad_ffn_gain: float32 [1024], replicated
- grad_gate_weight: float32 [1024, 4608], P('seq', 'head')
- grad_up_weight: float32 [1024, 4608], P('seq', 'head')
- grad_down_weight: float32 [1024, 4608], P('seq', 'head')
Inputs may be any that keep to these rules, and one draw needn't show every extreme that they name: `segment_ids`: ids start at 0, never fall along the tokens and rise by one at each sequence boundary; the tokens of one id form one sequence of at most 4096 tokens.
All inputs are finite; a program needn't handle non-finite values.
Results may differ from a plain program's by a relative error of at most 0.0095.
Values sent between devices are 32-bit elements; how exact they have to be, the bound alone decides.
A program may use at most 128 MiB of HBM per device.

v0:
```python
import jax
import jax.numpy as jnp
from jax import lax
from jax.sharding import PartitionSpec as P

EPS = 1e-05


def from_behind(block, axis, distance):
    devices = range(lax.axis_size(axis))
    route = [(i - distance, i) for i in devices if i - distance in devices]
    return lax.ppermute(block, axis, route)


def copy_for_each(x, axis):
    copies = jnp.broadcast_to(x, (lax.axis_size(axis), *x.shape))
    return lax.all_to_all(copies, axis, split_axis=0, concat_axis=0, tiled=True)


def of_everyone(x, axis):
    return copy_for_each(x, axis).sum(axis=0)


def in_one(arrays, axis):
    ends = [0]
    for a in arrays:
        ends.append(ends[-1] + a.size)
    so_far = of_everyone(jnp.concatenate([a.ravel() for a in arrays]), axis)
    return tuple((so_far[b:e].reshape(a.shape) for a, b, e in zip(arrays, ends, ends[1:])))


def in_one_piece(arrays, axis, dim, along):
    columns = [a.reshape(*a.shape[:along], -1) for a in arrays]
    both = jnp.concatenate(columns, axis=along)
    whole, at, finished = (lax.psum_scatter(both, axis, scatter_dimension=dim, tiled=True), 0, [])
    for a, column in zip(arrays, columns):
        piece = whole[..., at : at + column.shape[along]]
        finished.append(piece.reshape(*piece.shape[:along], *a.shape[along:]))
        at += column.shape[along]
    return tuple(finished)


def rms_scale(values):
    return lax.rsqrt(jnp.mean(values * values, axis=-1, keepdims=True) + EPS)


def norm_back(grad_normed, values, scale, gain):
    weighted = grad_normed * gain
    inner = jnp.mean(weighted * values, axis=-1, keepdims=True)
    grad_values = scale * weighted - values * (scale * scale * scale) * inner
    gain_grad = jnp.sum(grad_normed * values * scale, axis=0)
    return (grad_values, gain_grad)


def right_product(left, right):
    return lax.dot_general(
        left, right, (((1,), (1,)), ((), ())), preferred_element_type=jnp.float32
    )


def token_product(left, right):
    return lax.dot_general(
        left, right, (((0,), (0,)), ((), ())), preferred_element_type=jnp.float32
    )


def on_device(
    tokens,
    segment_ids,
    mix_gain,
    in_weight,
    conv_weight,
    out_weight,
    ffn_gain,
    gate_weight,
    up_weight,
    down_weight,
    cotangent,
):
    tok_rows = tokens.shape[0]
    first_row = lax.axis_index("seq") * tok_rows
    padded_ids = jnp.concatenate(
        [jnp.full((2,), -1, jnp.int32), segment_ids, jnp.full((2,), -2, jnp.int32)]
    )
    id_window = lax.dynamic_slice_in_dim(padded_ids, first_row, tok_rows + 4)
    near_ext = (id_window[2 : tok_rows + 4] == id_window[1 : tok_rows + 3]).astype(jnp.float32)
    far_ext = (id_window[2 : tok_rows + 4] == id_window[0 : tok_rows + 2]).astype(jnp.float32)
    near_own = near_ext[:tok_rows, None]
    far_own = far_ext[:tok_rows, None]
    inputs = tokens.astype(jnp.float32)
    mix_scale = rms_scale(inputs)
    mix_normed = (inputs * mix_scale * mix_gain).astype(jnp.bfloat16)
    projected = jnp.einsum("td,dkc->tkc", mix_normed, in_weight, preferred_element_type=jnp.float32)
    chan_b = projected[:, 0]
    chan_c = projected[:, 1]
    chan_x = projected[:, 2]
    mixed = chan_b * chan_x
    edge_rows = from_behind(mixed[tok_rows - 2 :], "seq", 1)
    extended = jnp.concatenate([edge_rows, mixed])
    kernel = conv_weight.astype(jnp.float32)
    prev_one = extended[1 : tok_rows + 1]
    prev_two = extended[0:tok_rows]
    conv_out = kernel[0] * mixed + kernel[1] * near_own * prev_one + kernel[2] * far_own * prev_two
    gated = (chan_c * conv_out).astype(jnp.bfloat16)
    resid = inputs + lax.psum(right_product(gated, out_weight), "head")
    ffn_scale = rms_scale(resid)
    ffn_normed = (resid * ffn_scale * ffn_gain).astype(jnp.bfloat16)
    gate = jnp.dot(ffn_normed, gate_weight, preferred_element_type=jnp.float32)
    upper = jnp.dot(ffn_normed, up_weight, preferred_element_type=jnp.float32)
    sigma = jax.nn.sigmoid(gate)
    act = (gate * sigma * upper).astype(jnp.bfloat16)
    result = (resid + lax.psum(right_product(act, down_weight), "head")).astype(jnp.bfloat16)
    d_act = jnp.dot(cotangent, down_weight, preferred_element_type=jnp.float32)
    d_gate = (d_act * upper * sigma * (1.0 + gate * (1.0 - sigma))).astype(jnp.bfloat16)
    d_up = (d_act * gate * sigma).astype(jnp.bfloat16)
    grad_down = token_product(cotangent, act)
    grad_gate = token_product(ffn_normed, d_gate)
    grad_up = token_product(ffn_normed, d_up)
    d_normed = lax.psum(right_product(d_gate, gate_weight) + right_product(d_up, up_weight), "head")
    d_hidden, grad_ffn_gain = norm_back(d_normed, resid, ffn_scale, ffn_gain)
    d_resid = d_hidden + cotangent.astype(jnp.float32)
    d_resid_low = d_resid.astype(jnp.bfloat16)
    d_gated = jnp.dot(d_resid_low, out_weight, preferred_element_type=jnp.float32)
    grad_out = token_product(d_resid_low, gated)
    d_chan_c = d_gated * conv_out
    d_conv = d_gated * chan_c
    tail_rows = from_behind(d_conv[:2], "seq", -1)
    later = jnp.concatenate([d_conv, tail_rows])
    d_mixed = (
        kernel[0] * d_conv
        + kernel[1] * near_ext[1 : tok_rows + 1, None] * later[1 : tok_rows + 1]
        + kernel[2] * far_ext[2 : tok_rows + 2, None] * later[2 : tok_rows + 2]
    )
    grad_conv = jnp.stack(
        [
            jnp.sum(d_conv * mixed, axis=0),
            jnp.sum(d_conv * near_own * prev_one, axis=0),
            jnp.sum(d_conv * far_own * prev_two, axis=0),
        ]
    )
    d_projected = jnp.stack([d_mixed * chan_x, d_chan_c, d_mixed * chan_b], axis=1).astype(
        jnp.bfloat16
    )
    grad_in = jnp.einsum("td,tkc->dkc", mix_normed, d_projected, preferred_element_type=jnp.float32)
    d_mix_normed = lax.psum(
        jnp.einsum("tkc,dkc->td", d_projected, in_weight, preferred_element_type=jnp.float32),
        "head",
    )
    d_inputs, grad_mix_gain = norm_back(d_mix_normed, inputs, mix_scale, mix_gain)
    grad_tokens = d_resid + d_inputs
    conv_total, gain_totals = in_one((grad_conv, jnp.stack([grad_mix_gain, grad_ffn_gain])), "seq")
    in_share, out_share, gate_share, up_share, down_share = in_one_piece(
        (grad_in, grad_out, grad_gate, grad_up, grad_down), "seq", 0, 1
    )
    return (
        result,
        grad_tokens,
        gain_totals[0],
        in_share,
        conv_total,
        out_share,
        gain_totals[1],
        gate_share,
        up_share,
        down_share,
    )


def solution(mesh):
    placed = (
        P("seq", None),
        P(),
        P(),
        P(None, None, "head"),
        P(None, "head"),
        P(None, "head"),
        P(),
        P(None, "head"),
        P(None, "head"),
        P(None, "head"),
        P("seq", None),
    )
    return jax.shard_map(
        on_device,
        mesh=mesh,
        in_specs=placed,
        out_specs=(
            P("seq", None),
            P("seq", None),
            P(),
            P("seq", None, "head"),
            P(None, "head"),
            P("seq", "head"),
            P(),
            P("seq", "head"),
            P("seq", "head"),
            P("seq", "head"),
        ),
        check_vma=False,
    )
```

profile of v0, /device:TPU:0, one launch (start us, length us, event | category | flops | bytes accessed | tf_op | source)
XLA Modules:
  0.0 405.6 jit_solution(4112243098430087586)
XLA Ops:
  8.9 2.8 fusion.12
  15.2 2.2 multiply_convert_fusion.7
  18.1 2.9 fusion.39
  21.1 64.1 %all-reduce.5.cloned.1.call-done = f32[512,1024]{1,0:T(8,128)} async-done(((f32[512,1024]{1,0:T(8,128)}), f32[512,1024]{1,0:T(8,128)}) %all-reduce.5.cloned.1.call-update) | async-done | bytes 2097168 | tf_op jit(solution)/shard_map/psum | solution.py:105
  85.1 1.9 multiply_reduce_fusion.2
  87.4 2.1 copy-done.32
  93.1 3.3 multiply_convert_fusion
  98.0 2.9 convolution_add_fusion
  101.0 58.6 %all-reduce.7.cloned.1.call-done = f32[512,1024]{1,0:T(8,128)} async-done(((f32[512,1024]{1,0:T(8,128)}), f32[512,1024]{1,0:T(8,128)}) %all-reduce.7.cloned.1.call-update) | async-done | bytes 2097168 | tf_op jit(solution)/shard_map/psum | solution.py:119
  159.6 2.9 multiply_reduce_fusion
  169.2 2.9 fusion.42
  173.5 2.4 convolution_bitcast_fusion
  176.9 2.7 fusion.10
  179.6 3.6 copy.39
  183.2 4.3 %constant_dynamic-update-slice_fusion = f32[1024,4480]{1,0:T(8,128)} fusion(f32[1024,768]{1,0:T(8,128)} %copy.39), kind=kLoop, calls=%fused_computation.68 | loop fusion | bytes 6291456
  189.4 4.0 convolution_dynamic-update-slice_fusion.1
  193.5 3.8 convolution_dynamic-update-slice_fusion
  197.3 3.9 bitcast_dynamic-update-slice_fusion
  201.2 68.6 %all-reduce.9.cloned.1.call-done = (f32[512,1024]{1,0:T(8,128)}, f32[512,1024]{1,0:T(8,128)}) async-done(((f32[512,1024]{1,0:T(8,128)}, f32[512,1024]{1,0:T(8,128)}), (f32[512,1024]{1,0:T(8,128)}, f32[512,1024]{1,0:T(8,128)})) %all-reduce.9.cloned.1.call-update) | async-done | bytes 4194320 | tf_op jit(solution)/shard_map/psum | solution.py:112
  269.8 2.3 fusion.8
  273.1 7.3 %all-to-all-start = ((f32[32,1,2816]{2,1,0:T(1,128)}), f32[32,1,2816]{2,1,0:T(1,128)}, u32[]{:S(2)}, u32[]{:S(2)}) async-start(f32[32,1,2816]{2,1,0:T(1,128)} %broadcast_in_dim.2), calls=%async_computation | async-start | bytes 720896 | tf_op jit(solution)/shard_map/all_to_all | solution.py:17
  280.5 3.6 fusion.5
  285.4 4.7 %all-to-all-done = f32[32,1,2816]{2,1,0:T(1,128)} async-done(((f32[32,1,2816]{2,1,0:T(1,128)}), f32[32,1,2816]{2,1,0:T(1,128)}, u32[]{:S(2)}, u32[]{:S(2)}) %all-to-all-start) | async-done | bytes 360480 | tf_op jit(solution)/shard_map/all_to_all | solution.py:17
  292.6 101.8 %reduce-scatter.2.cloned.1.call-done = f32[32,4480]{1,0:T(8,128)} async-done(((f32[1024,4480]{1,0:T(8,128)}), f32[32,4480]{1,0:T(8,128)}) %reduce-scatter.2.cloned.1.call-update) | async-done | bytes 573456 | tf_op jit(solution)/shard_map/reduce_scatter | solution.py:35
  (125 shorter events, 31.7 us)
Async XLA Ops:
  7.2 85.9 %copy-start = (bf16[1024,1152]{1,0:T(8,128)(2,1)S(1)}, bf16[1024,1152]{1,0:T(8,128)(2,1)}, u32[]{:S(2)}) copy-start(bf16[1024,1152]{1,0:T(8,128)(2,1)} %param.20) | copy-start | bytes 7077892
  7.2 78.0 %all-reduce.5.cloned.1.call-start = ((), (), s32[]{:S(2)}) async-start(), calls=%async_computation.2 | async-start | bytes 4194304 | tf_op jit(solution)/shard_map/psum | solution.py:105
  8.9 5.5 %copy-start.28 = (s32[16384]{0:T(1024)S(1)}, s32[16384]{0:T(1024)}, u32[]{:S(2)}) copy-start(s32[16384]{0:T(1024)} %param.12) | copy-start | bytes 196612
  8.9 5.8 %copy-start.31 = (bf16[3,256]{1,0:T(4,128)(2,1)S(1)}, bf16[3,256]{1,0:T(4,128)(2,1)}, u32[]{:S(2)}) copy-start(bf16[3,256]{1,0:T(4,128)(2,1)} %param.15) | copy-start | bytes 4612
  13.0 4.3 %copy-start.13 = (f32[512,256]{1,0:T(8,128)}, f32[512,256]{1,0:T(8,128)S(1)}, u32[]{:S(2)}) copy-start(f32[512,256]{1,0:T(8,128)S(1)} %fusion.24) | copy-start | bytes 1572868
  13.1 2.1 collective-permute-start
  18.1 67.1 %copy-start.7 = (bf16[512,1024]{1,0:T(8,128)(2,1)S(1)}, bf16[512,1024]{1,0:T(8,128)(2,1)}, u32[]{:S(2)}) copy-start(bf16[512,1024]{1,0:T(8,128)(2,1)} %param.11) | copy-start | bytes 3145732
  21.0 66.1 %copy-start.29 = (f32[1024]{0:T(1024)S(1)}, f32[1024]{0:T(1024)}, u32[]{:S(2)}) copy-start(f32[1024]{0:T(1024)} %param.17) | copy-start | bytes 12292
  21.0 138.5 %all-reduce.7.cloned.1.call-start = ((), (), s32[]{:S(2)}) async-start(), calls=%async_computation.3 | async-start | bytes 4194304 | tf_op jit(solution)/shard_map/psum | solution.py:119
  87.1 4.0 copy-start.2
  100.9 168.9 %all-reduce.9.cloned.1.call-start = ((), (), s32[]{:S(2)}) async-start(), calls=%async_computation.5 | async-start | bytes 8388608 | tf_op jit(solution)/shard_map/psum | solution.py:112
  165.4 3.8 copy-start.35
  167.7 4.8 %copy-start.26 = (bf16[512,1,256]{2,0,1:T(8,128)(2,1)}, bf16[512,1,256]{2,0,1:T(8,128)(2,1)S(1)}, u32[]{:S(2)}) copy-start(bf16[512,1,256]{2,0,1:T(8,128)(2,1)S(1)} %get-tuple-element.72) | copy-start | bytes 786436
  167.7 4.4 %collective-permute-start.1 = (f32[2,256]{1,0:T(2,128)S(1)}, f32[2,256]{1,0:T(2,128)S(1)}, u32[]{:S(2)}, u32[]{:S(2)}) collective-permute-start(f32[2,256]{1,0:T(2,128)S(1)} %slice.137), channel_id=1, source_target_pairs={{4,0},{8,4},{12,8},{16,12},{20,16},{24,20},{28,24},{32,28},{36,32}... | collective-permute-start | bytes 6152 | tf_op jit(solution)/shard_map/ppermute | solution.py:12
  176.0 218.4 %reduce-scatter.2.cloned.1.call-start = ((), (), s32[]{:S(2)}) async-start(), calls=%async_computation.4 | async-start | bytes 18923520 | tf_op jit(solution)/shard_map/reduce_scatter | solution.py:35
  183.2 4.3 %copy-start.6 = (f32[512,1024]{1,0:T(8,128)S(1)}, f32[512,1024]{1,0:T(8,128)}, u32[]{:S(2)}) copy-start(f32[512,1024]{1,0:T(8,128)} %copy-done.5) | copy-start | bytes 6291460
  183.2 4.3 %copy-start.16 = (bf16[512,256]{1,0:T(8,128)(2,1)S(1)}, bf16[512,256]{1,0:T(8,128)(2,1)}, u32[]{:S(2)}) copy-start(bf16[512,256]{1,0:T(8,128)(2,1)} %copy-done.15) | copy-start | bytes 786436
  189.4 4.0 copy-start.21
  193.5 3.8 copy-start.25
  193.5 3.8 copy-start.36
  273.1 17.0 %all-to-all-start = ((f32[32,1,2816]{2,1,0:T(1,128)}), f32[32,1,2816]{2,1,0:T(1,128)}, u32[]{:S(2)}, u32[]{:S(2)}) async-start(f32[32,1,2816]{2,1,0:T(1,128)} %broadcast_in_dim.2), calls=%async_computation | async-start | bytes 720896 | tf_op jit(solution)/shard_map/all_to_all | solution.py:17
  280.5 3.6 copy-start.4
  280.5 3.6 copy-start.17
  284.1 115.0 %copy-start.1 = (bf16[1024,1152]{1,0:T(8,128)(2,1)S(1)}, bf16[1024,1152]{1,0:T(8,128)(2,1)}, u32[]{:S(2)}) copy-start(bf16[1024,1152]{1,0:T(8,128)(2,1)} %param.20) | copy-start | bytes 7077892
  (20 other events, 37.4 us)
Sparse Core Ops, SparseCore 0:
  21.1 63.9 all-reduce.4
  101.0 58.4 all-reduce.6
  176.1 93.6 all-reduce.8
  274.2 120.0 reduce-scatter.1
where the time goes:
time: 406 us
  waiting for transfers between devices  298 us (73%)
  matrix products  38.2 us (9%)
  local copies, waits for them, and re-layouts  24.5 us (6%)
  other arithmetic  20.2 us (5%)
  between operations  14.2 us (3%)
  starting transfers between devices  10.3 us (3%)
    reduce_scatter x1, waiting for transfers between devices, in_one_piece(): lax.psum_scatter(both, axis, scatter_dimension=dim, tiled=True)  102 us
    psum x1, waiting for transfers between devices, on_device(): lax.psum(right_product(act, down_weight), 'head')  68.6 us
    psum x1, waiting for transfers between devices, on_device(): resid = inputs + lax.psum(right_product(gated, out_weight), 'head')  64.1 us
    psum x1, waiting for transfers between devices, on_device(): lax.psum(right_product(d_gate, gate_weight) + right_product(d_up, up_weig...  58.6 us
    unnamed x76, local copies, waits for them, and re-layouts  13.7 us
    dot_general x4, matrix products, token_product(): lax.dot_general(left, right, (((0,), (0,)), ((), ())), preferred_element_...  13.2 us
    dot_general x4, matrix products, right_product(): lax.dot_general(left, right, (((1,), (1,)), ((), ())), preferred_element_...  10.2 us
  transfers between devices with their start and end apart: 7, of which 6 were waited for; matrix products, arithmetic and copies ran while one was open for 9% of the time, Pallas kernels for 0%

commit v1 on v0

--- a/solution.py
+++ b/solution.py
@@ -116,7 +116,10 @@
     grad_down = token_product(cotangent, act)
     grad_gate = token_product(ffn_normed, d_gate)
     grad_up = token_product(ffn_normed, d_up)
-    d_normed = lax.psum(right_product(d_gate, gate_weight) + right_product(d_up, up_weight), "head")
+    d_normed = jnp.sum(
+        lax.all_gather(right_product(d_gate, gate_weight) + right_product(d_up, up_weight), "head"),
+        axis=0,
+    )
     d_hidden, grad_ffn_gain = norm_back(d_normed, resid, ffn_scale, ffn_gain)
     d_resid = d_hidden + cotangent.astype(jnp.float32)
     d_resid_low = d_resid.astype(jnp.bfloat16)

time: 406 us -> 437 us (1.076)
  waiting for transfers between devices: 298 us -> 323 us
  other arithmetic: 20.2 us -> 26.4 us
    all_gather x0 -> x1, waiting for transfers between devices: none -> 82.9 us  [on_device(): lax.all_gather(right_product(d_gate, gate_weight) + right_product(d_up, u...]
    psum x1 -> x0, waiting for transfers between devices: 58.6 us -> none  [on_device(): lax.psum(right_product(d_gate, gate_weight) + right_product(d_up, up_weig...]
    reduce_sum x0 -> x1, other arithmetic: none -> 5.88 us  [on_device(): jnp.sum(lax.all_gather(right_product(d_gate, gate_weight) + right_product...]
where the time goes in v1:
time: 437 us
  waiting for transfers between devices  323 us (74%)
  matrix products  38.2 us (9%)
  other arithmetic  26.4 us (6%)
  local copies, waits for them, and re-layouts  24 us (5%)
  between operations  14.2 us (3%)
  starting transfers between devices  10.5 us (2%)
    reduce_scatter x1, waiting for transfers between devices, in_one_piece(): lax.psum_scatter(both, axis, scatter_dimension=dim, tiled=True)  101 us
    all_gather x1, waiting for transfers between devices, on_device(): lax.all_gather(right_product(d_gate, gate_weight) + right_product(d_up, u...  82.9 us
    psum x1, waiting for transfers between devices, on_device(): lax.psum(right_product(act, down_weight), 'head')  70.2 us
    psum x1, waiting for transfers between devices, on_device(): resid = inputs + lax.psum(right_product(gated, out_weight), 'head')  64.1 us
    unnamed x76, local copies, waits for them, and re-layouts  13.3 us
    dot_general x4, matrix products, token_product(): lax.dot_general(left, right, (((0,), (0,)), ((), ())), preferred_element_...  13.2 us
    dot_general x4, matrix products, right_product(): lax.dot_general(left, right, (((1,), (1,)), ((), ())), preferred_element_...  10.2 us
  transfers between devices with their start and end apart: 7, of which 6 were waited for; matrix products, arithmetic and copies ran while one was open for 9% of the time, Pallas kernels for 0%

profile of v1, /device:TPU:0, one launch (start us, length us, event | category | flops | bytes accessed | tf_op | source)
XLA Modules:
  0.0 436.6 jit_solution(3690214051269826683)
XLA Ops:
  8.9 2.8 fusion.12
  15.2 2.2 multiply_convert_fusion.7
  18.1 2.9 fusion.39
  21.1 64.1 %all-reduce.4.cloned.1.call-done = f32[512,1024]{1,0:T(8,128)} async-done(((f32[512,1024]{1,0:T(8,128)}), f32[512,1024]{1,0:T(8,128)}) %all-reduce.4.cloned.1.call-update) | async-done | bytes 2097168 | tf_op jit(solution)/shard_map/psum | solution.py:105
  87.4 2.1 copy-done.32
  93.1 3.3 multiply_convert_fusion
  98.0 2.9 convolution_add_fusion
  101.1 82.9 %all-gather.3.cloned.1.call-done = f32[2048,1024]{1,0:T(8,128)} async-done(((f32[512,1024]{1,0:T(8,128)}), f32[2048,1024]{1,0:T(8,128)}) %all-gather.3.cloned.1.call-update) | async-done | bytes 8388624 | tf_op jit(solution)/shard_map/all_gather | solution.py:120
  184.0 5.9 %reduce_sum.101 = f32[512,1024]{1,0:T(8,128)} reduce(f32[4,512,1024]{2,1,0:T(8,128)} %bitcast.80, f32[]{:T(128)} %constant.6.clone.1), dimensions={0}, to_apply=%region_4.0 | reduce | flops 1572864 | bytes 10485764 | tf_op jit(solution)/shard_map/reduce_sum | solution.py:119
  189.9 2.9 multiply_reduce_fusion
  199.4 2.9 fusion.42
  203.7 2.4 convolution_bitcast_fusion
  207.1 2.7 fusion.10
  209.8 3.6 copy.39
  213.4 4.0 constant_dynamic-update-slice_fusion
  219.4 4.0 convolution_dynamic-update-slice_fusion.1
  223.4 3.8 convolution_dynamic-update-slice_fusion
  227.2 3.9 bitcast_dynamic-update-slice_fusion
  231.1 70.2 %all-reduce.6.cloned.1.call-done = (f32[512,1024]{1,0:T(8,128)}, f32[512,1024]{1,0:T(8,128)}) async-done(((f32[512,1024]{1,0:T(8,128)}, f32[512,1024]{1,0:T(8,128)}), (f32[512,1024]{1,0:T(8,128)}, f32[512,1024]{1,0:T(8,128)})) %all-reduce.6.cloned.1.call-update) | async-done | bytes 4194320 | tf_op jit(solution)/shard_map/psum | solution.py:112
  301.3 2.3 fusion.8
  304.6 7.3 %all-to-all-start = ((f32[32,1,2816]{2,1,0:T(1,128)}), f32[32,1,2816]{2,1,0:T(1,128)}, u32[]{:S(2)}, u32[]{:S(2)}) async-start(f32[32,1,2816]{2,1,0:T(1,128)} %broadcast_in_dim.2), calls=%async_computation | async-start | bytes 720896 | tf_op jit(solution)/shard_map/all_to_all | solution.py:17
  312.0 4.0 fusion.5
  317.3 4.4 all-to-all-done
  324.1 101.2 %reduce-scatter.2.cloned.1.call-done = f32[32,4480]{1,0:T(8,128)} async-done(((f32[1024,4480]{1,0:T(8,128)}), f32[32,4480]{1,0:T(8,128)}) %reduce-scatter.2.cloned.1.call-update) | async-done | bytes 573456 | tf_op jit(solution)/shard_map/reduce_scatter | solution.py:35
  (126 shorter events, 33.7 us)
Async XLA Ops:
  7.2 85.9 %copy-start = (bf16[1024,1152]{1,0:T(8,128)(2,1)S(1)}, bf16[1024,1152]{1,0:T(8,128)(2,1)}, u32[]{:S(2)}) copy-start(bf16[1024,1152]{1,0:T(8,128)(2,1)} %param.20) | copy-start | bytes 7077892
  7.2 78.0 %all-reduce.4.cloned.1.call-start = ((), (), s32[]{:S(2)}) async-start(), calls=%async_computation.2 | async-start | bytes 4194304 | tf_op jit(solution)/shard_map/psum | solution.py:105
  8.9 5.5 %copy-start.28 = (s32[16384]{0:T(1024)S(1)}, s32[16384]{0:T(1024)}, u32[]{:S(2)}) copy-start(s32[16384]{0:T(1024)} %param.12) | copy-start | bytes 196612
  8.9 5.8 %copy-start.31 = (bf16[3,256]{1,0:T(4,128)(2,1)S(1)}, bf16[3,256]{1,0:T(4,128)(2,1)}, u32[]{:S(2)}) copy-start(bf16[3,256]{1,0:T(4,128)(2,1)} %param.15) | copy-start | bytes 4612
  13.0 4.3 copy-start.13
  13.1 2.1 collective-permute-start
  18.1 67.1 %copy-start.8 = (bf16[512,1024]{1,0:T(8,128)(2,1)S(1)}, bf16[512,1024]{1,0:T(8,128)(2,1)}, u32[]{:S(2)}) copy-start(bf16[512,1024]{1,0:T(8,128)(2,1)} %param.11) | copy-start | bytes 3145732
  21.0 66.1 %copy-start.29 = (f32[1024]{0:T(1024)S(1)}, f32[1024]{0:T(1024)}, u32[]{:S(2)}) copy-start(f32[1024]{0:T(1024)} %param.17) | copy-start | bytes 12292
  21.0 163.0 %all-gather.3.cloned.1.call-start = ((), (), s32[]{:S(2)}) async-start(), calls=%async_computation.4 | async-start | bytes 10485760 | tf_op jit(solution)/shard_map/all_gather | solution.py:120
  87.1 4.0 copy-start.2
  100.9 200.4 %all-reduce.6.cloned.1.call-start = ((), (), s32[]{:S(2)}) async-start(), calls=%async_computation.5 | async-start | bytes 8388608 | tf_op jit(solution)/shard_map/psum | solution.py:112
  195.8 3.6 copy-start.35
  198.1 4.6 %copy-start.26 = (bf16[512,1,256]{2,0,1:T(8,128)(2,1)}, bf16[512,1,256]{2,0,1:T(8,128)(2,1)S(1)}, u32[]{:S(2)}) copy-start(bf16[512,1,256]{2,0,1:T(8,128)(2,1)S(1)} %get-tuple-element.72) | copy-start | bytes 786436
  198.1 4.2 collective-permute-start.1
  206.1 219.2 %reduce-scatter.2.cloned.1.call-start = ((), (), s32[]{:S(2)}) async-start(), calls=%async_computation.3 | async-start | bytes 18923520 | tf_op jit(solution)/shard_map/reduce_scatter | solution.py:35
  213.4 4.0 copy-start.6
  213.4 4.0 copy-start.16
  219.4 4.0 copy-start.21
  223.4 3.8 copy-start.25
  223.4 3.8 copy-start.36
  304.6 17.0 %all-to-all-start = ((f32[32,1,2816]{2,1,0:T(1,128)}), f32[32,1,2816]{2,1,0:T(1,128)}, u32[]{:S(2)}, u32[]{:S(2)}) async-start(f32[32,1,2816]{2,1,0:T(1,128)} %broadcast_in_dim.2), calls=%async_computation | async-start | bytes 720896 | tf_op jit(solution)/shard_map/all_to_all | solution.py:17
  312.0 4.0 copy-start.4
  312.0 4.0 copy-start.17
  316.0 114.1 %copy-start.1 = (bf16[1024,1152]{1,0:T(8,128)(2,1)S(1)}, bf16[1024,1152]{1,0:T(8,128)(2,1)}, u32[]{:S(2)}) copy-start(bf16[1024,1152]{1,0:T(8,128)(2,1)} %param.20) | copy-start | bytes 7077892
  (20 other events, 37.4 us)
Sparse Core Ops, SparseCore 0:
  21.1 63.9 all-reduce.3
  101.0 82.9 all-gather.2
  206.3 95.0 all-reduce.5
  305.2 120.0 reduce-scatter.1
